TPU v7x, 32 devices: a whole 2x2x4 slice. The times are simulated.
32 devices in a mesh: dp: 16 (over z, y, x), rep: 2 (over core).
Axes of the slice: x: 2, y: 2, z: 4, core: 2. Of those that a mesh axis runs over, the one named last changes fastest.
Arguments:
- table: float32 [131072, 400], P(('dp', 'rep')), may hold values from -6 to 6
- batch_index: int32 [32768], P(('dp', 'rep')), may hold values from 0 to 4095
- labels: int32 [32768], P(('dp', 'rep')), may hold values from 0 to 46
- w_branch: float32 [4, 100, 512], P(None, None, 'dp'), may hold values from -0.625 to 0.625
- w_merge: float32 [2048, 512], P('dp'), may hold values from -0.125 to 0.125
- w_class: float32 [512, 47], P('dp'), may hold values from -0.5 to 0.5
- small_params: float32 [20, 512], P(None, 'dp'), as said below
- first_branch: float32 [4, 100, 512], P(None, None, 'dp'), may hold values from -0.0014648438 to 0.0014648438
- first_merge: float32 [2048, 512], P('dp'), may hold values from -0.0014648438 to 0.0014648438
- first_class: float32 [512, 47], P('dp'), may hold values from -0.0014648438 to 0.0014648438
- first_small: float32 [20, 512], P(None, 'dp'), may hold values from -0.00390625 to 0.00390625
- second_branch: float32 [4, 100, 512], P(None, None, 'dp'), may hold values from 7.7659046e-10 to 3.1063618e-09
- second_merge: float32 [2048, 512], P('dp'), may hold values from 7.7659046e-10 to 3.1063618e-09
- second_class: float32 [512, 47], P('dp'), may hold values from 7.7659046e-10 to 3.1063618e-09
- second_small: float32 [20, 512], P(None, 'dp'), may hold values from 6.989314e-09 to 2.7957256e-08
Outputs:
- new_branch: float32 [4, 100, 512], P(None, None, 'dp')
- new_merge: float32 [2048, 512], P('dp')
- new_class: float32 [512, 47], P('dp')
- new_small: float32 [20, 512], P(None, 'dp')
- moment_branch: float32 [4, 100, 512], P(None, None, 'dp')
- moment_merge: float32 [2048, 512], P('dp')
- moment_class: float32 [512, 47], P('dp')
- moment_small: float32 [20, 512], P(None, 'dp')
- square_branch: float32 [4, 100, 512], P(None, None, 'dp')
- square_merge: float32 [2048, 512], P('dp')
- square_class: float32 [512, 47], P('dp')
- square_small: float32 [20, 512], P(None, 'dp')
- copy_branch: bfloat16 [4, 100, 512], P(None, None, 'dp')
- copy_merge: bfloat16 [2048, 512], P('dp')
- copy_class: bfloat16 [512, 47], P('dp')
- copy_small: bfloat16 [20, 512], P(None, 'dp')
- grad_norm: float32 [], replicated
- row_grads: float32 [32768, 400], P(('dp', 'rep'))
Inputs may be any that keep to these rules, and one draw needn't show every extreme that they name: `batch_index`: each entry indexes a row of the block of 4096 table rows that lies on the same device as the entry. `small_params`: gains lie in 0.3 to 2.0, slopes in 0.05 to 0.45.
All inputs are finite; a program needn't handle non-finite values.
Results may differ from a plain program's by a relative error of at most 0.011.
Values may be sent and summed in bfloat16 or wider, within the bound.
No kernel may reach another device: no remote copies, remote signals or barrier semaphores. Data moves between devices by JAX's collectives and lax.ppermute only.
A program may use at most 128 MiB of HBM per device.

v0:
```python
import jax
import jax.numpy as jnp
from jax import lax
from jax.sharding import PartitionSpec as P

HOPS = 4
STEP = 7
EPS_NORM = 1e-05


def leaky(value, slope):
    return slope * value + (1.0 - slope) * value * jax.nn.sigmoid(value)


def leaky_back(upstream, value, slope):
    sig = jax.nn.sigmoid(value)
    slope_term = jnp.sum(upstream * value * (1.0 - sig), axis=0)
    derivative = slope + (1.0 - slope) * (sig + value * sig * (1.0 - sig))
    return (upstream * derivative, slope_term)


def cross_dot(left, right):
    return lax.dot_general(
        left, right, (((0,), (0,)), ((), ())), preferred_element_type=jnp.float32
    )


def back_dot(left, right):
    return lax.dot_general(
        left, right, (((1,), (1,)), ((), ())), preferred_element_type=jnp.float32
    )


def adamw(weight, grad, moment, square, scale, rate):
    clipped = grad * scale
    moment_new = 0.9 * moment + 0.1 * clipped
    square_new = 0.999 * square + 0.001 * clipped * clipped
    fix_one = 1.0 - 0.9**STEP
    fix_two = 1.0 - 0.999**STEP
    update = moment_new / fix_one / (jnp.sqrt(square_new / fix_two) + 1e-08) + 0.01 * weight
    weight_new = weight - rate * update
    return (weight_new, moment_new, square_new)


def on_device(
    table,
    batch_index,
    labels,
    w_branch,
    w_merge,
    w_class,
    small_params,
    first_branch,
    first_merge,
    first_class,
    first_small,
    second_branch,
    second_merge,
    second_class,
    second_small,
):
    batch = batch_index.shape[0]
    row_count = batch * lax.axis_size("dp") * lax.axis_size("rep")
    d_in = w_branch.shape[1]
    hidden = w_merge.shape[1]
    hidden_width = HOPS * hidden
    classes = w_class.shape[1]
    rows = jnp.take(table, batch_index, axis=0)
    input_features = rows.astype(jnp.bfloat16).reshape(batch, HOPS, d_in)
    branch_full, merge_full, class_full, small_full = (
        lax.all_gather(w_branch.astype(jnp.bfloat16), "dp", axis=2, tiled=True),
        lax.all_gather(w_merge.astype(jnp.bfloat16), "dp", axis=0, tiled=True),
        lax.all_gather(w_class.astype(jnp.bfloat16), "dp", axis=0, tiled=True),
        lax.all_gather(small_params.astype(jnp.bfloat16), "dp", axis=1, tiled=True),
    )
    params = small_full.astype(jnp.float32)
    gain1 = params[0:HOPS].reshape(hidden_width)
    shift1 = params[HOPS : 2 * HOPS].reshape(hidden_width)
    slope1 = params[2 * HOPS : 3 * HOPS].reshape(hidden_width)
    slope_join = params[3 * HOPS : 4 * HOPS].reshape(hidden_width)
    gain2 = params[4 * HOPS]
    shift2 = params[4 * HOPS + 1]
    slope2 = params[4 * HOPS + 2]
    bias3 = params[4 * HOPS + 3, :classes]
    first_pre = jnp.einsum(
        "fsq,sqv->fsv", input_features, branch_full, preferred_element_type=jnp.float32
    ).reshape(batch, hidden_width)
    sums_one = lax.psum(
        (jnp.sum(first_pre, axis=0), jnp.sum(first_pre * first_pre, axis=0)), ("dp", "rep")
    )
    mean1 = sums_one[0] / row_count
    inv1 = lax.rsqrt(sums_one[1] / row_count - mean1 * mean1 + EPS_NORM)
    norm1 = (first_pre - mean1) * inv1
    lin1 = gain1 * norm1 + shift1
    act1 = leaky(lin1, slope1)
    joined_low = leaky(act1, slope_join).astype(jnp.bfloat16)
    pre2 = jnp.dot(joined_low, merge_full, preferred_element_type=jnp.float32)
    sums_two = lax.psum((jnp.sum(pre2, axis=0), jnp.sum(pre2 * pre2, axis=0)), ("dp", "rep"))
    mean2 = sums_two[0] / row_count
    inv2 = lax.rsqrt(sums_two[1] / row_count - mean2 * mean2 + EPS_NORM)
    norm2 = (pre2 - mean2) * inv2
    lin2 = gain2 * norm2 + shift2
    act2_low = leaky(lin2, slope2).astype(jnp.bfloat16)
    logits = jnp.dot(act2_low, class_full, preferred_element_type=jnp.float32) + bias3
    probs = jax.nn.softmax(logits, axis=1)
    onehot = (labels[:, None] == jnp.arange(classes, dtype=jnp.int32)[None, :]).astype(jnp.float32)
    dlogits = (probs - onehot).astype(jnp.bfloat16)
    branch_back, merge_back, class_back = (
        lax.all_gather(w_branch.astype(jnp.bfloat16), "dp", axis=2, tiled=True),
        lax.all_gather(w_merge.astype(jnp.bfloat16), "dp", axis=0, tiled=True),
        lax.all_gather(w_class.astype(jnp.bfloat16), "dp", axis=0, tiled=True),
    )
    grad_class = cross_dot(act2_low, dlogits)
    grad_bias3 = jnp.sum(dlogits.astype(jnp.float32), axis=0)
    dact2 = back_dot(dlogits, class_back)
    dy2, grad_slope2 = leaky_back(dact2, lin2, slope2)
    gain2_part = jnp.sum(dy2 * norm2, axis=0)
    shift2_part = jnp.sum(dy2, axis=0)
    totals_two = lax.psum((shift2_part, gain2_part), ("dp", "rep"))
    dpre2 = (
        inv2
        * (
            gain2 * dy2
            - gain2 * totals_two[0] / row_count
            - norm2 * gain2 * totals_two[1] / row_count
        )
    ).astype(jnp.bfloat16)
    grad_merge = cross_dot(joined_low, dpre2)
    djoined = back_dot(dpre2, merge_back)
    dact1, grad_slope_join = leaky_back(djoined, act1, slope_join)
    dy1, grad_slope1 = leaky_back(dact1, lin1, slope1)
    gain1_part = jnp.sum(dy1 * norm1, axis=0)
    shift1_part = jnp.sum(dy1, axis=0)
    totals_one = lax.psum((shift1_part, gain1_part), ("dp", "rep"))
    first_grad = (
        inv1
        * (
            gain1 * dy1
            - gain1 * totals_one[0] / row_count
            - norm1 * gain1 * totals_one[1] / row_count
        )
    ).astype(jnp.bfloat16)
    first_grad = first_grad.reshape(batch, HOPS, hidden)
    branch_gradient = jnp.einsum(
        "pze,pzv->zev", input_features, first_grad, preferred_element_type=jnp.float32
    )
    row_grads = jnp.einsum(
        "fsz,sez->fse", first_grad, branch_back, preferred_element_type=jnp.float32
    ).reshape(batch, HOPS * d_in)
    bias_row = jnp.zeros((hidden,), jnp.float32).at[:classes].set(grad_bias3)
    grad_small = jnp.concatenate(
        [
            gain1_part.reshape(HOPS, hidden),
            shift1_part.reshape(HOPS, hidden),
            grad_slope1.reshape(HOPS, hidden),
            grad_slope_join.reshape(HOPS, hidden),
            gain2_part[None],
            shift2_part[None],
            grad_slope2[None],
            bias_row[None],
        ],
        axis=0,
    )
    paired = (
        lax.psum(branch_gradient.astype(jnp.bfloat16), "rep").astype(jnp.float32),
        lax.psum(grad_merge.astype(jnp.bfloat16), "rep").astype(jnp.float32),
        lax.psum(grad_class.astype(jnp.bfloat16), "rep").astype(jnp.float32),
        lax.psum(grad_small.astype(jnp.bfloat16), "rep").astype(jnp.float32),
    )
    shares = (
        lax.psum_scatter(paired[0], "dp", scatter_dimension=2, tiled=True),
        lax.psum_scatter(paired[1], "dp", scatter_dimension=0, tiled=True),
        lax.psum_scatter(paired[2], "dp", scatter_dimension=0, tiled=True),
        lax.psum_scatter(paired[3], "dp", scatter_dimension=1, tiled=True),
    )
    local_squares = jnp.float32(0.0)
    for share in shares:
        local_squares = local_squares + jnp.sum(share * share)
    grad_norm = jnp.sqrt(lax.psum(local_squares, "dp"))
    scale = 1.0 / jnp.maximum(grad_norm, 1.0)
    weights = (w_branch, w_merge, w_class, small_params)
    firsts = (first_branch, first_merge, first_class, first_small)
    seconds = (second_branch, second_merge, second_class, second_small)
    rates = (0.05, 0.05, 0.05, 0.3)
    results = [
        adamw(w, g, m, v, scale, r)
        for w, g, m, v, r in zip(weights, shares, firsts, seconds, rates)
    ]
    news = tuple((r[0] for r in results))
    moments = tuple((r[1] for r in results))
    squares = tuple((r[2] for r in results))
    copies = tuple((r.astype(jnp.bfloat16) for r in news))
    return (
        news[0],
        news[1],
        news[2],
        news[3],
        moments[0],
        moments[1],
        moments[2],
        moments[3],
        squares[0],
        squares[1],
        squares[2],
        squares[3],
        copies[0],
        copies[1],
        copies[2],
        copies[3],
        grad_norm,
        row_grads,
    )


def solution(mesh):
    placed = (
        P(("dp", "rep"), None),
        P(("dp", "rep")),
        P(("dp", "rep")),
        P(None, None, "dp"),
        P("dp", None),
        P("dp", None),
        P(None, "dp"),
        P(None, None, "dp"),
        P("dp", None),
        P("dp", None),
        P(None, "dp"),
        P(None, None, "dp"),
        P("dp", None),
        P("dp", None),
        P(None, "dp"),
    )
    return jax.shard_map(
        on_device,
        mesh=mesh,
        in_specs=placed,
        out_specs=(
            P(None, None, "dp"),
            P("dp", None),
            P("dp", None),
            P(None, "dp"),
            P(None, None, "dp"),
            P("dp", None),
            P("dp", None),
            P(None, "dp"),
            P(None, None, "dp"),
            P("dp", None),
            P("dp", None),
            P(None, "dp"),
            P(None, None, "dp"),
            P("dp", None),
            P("dp", None),
            P(None, "dp"),
            P(),
            P(("dp", "rep"), None),
        ),
        check_vma=False,
    )
```

profile of v0, /device:TPU:0, one launch (start us, length us, event | category | flops | bytes accessed | tf_op | source)
XLA Modules:
  0.0 804.2 jit_solution(16714491165405822003)
XLA Ops:
  7.2 1.6 convert_element_type.82
  8.9 0.0 all-reduce.10.cloned.1.call-start
  8.9 0.7 compare_and_fusion
  9.6 0.7 fusion.19
  10.3 0.7 convert_bitcast_fusion
  11.0 0.7 convert_element_type.84
  11.8 0.8 convert_element_type.78
  12.6 43.0 %all-gather = bf16[16,32,20]{1,2,0:T(8,128)(2,1)S(1)} all-gather(bf16[1,32,20]{1,2,0:T(8,128)(2,1)S(1)} %convert_bitcast_fusion), channel_id=1, replica_groups=mesh['dp'=16,'rep'=2] {'dp'}, dimensions={0}, use_global_device_ids=true | all-gather | bytes 21760 | tf_op jit(solution)/shard_map/all_gather | solution.py:74
  55.6 0.1 reshape.147
  55.8 40.4 %all_gather.15 = bf16[4,100,512]{1,2,0:T(8,128)(2,1)S(1)} all-gather(bf16[4,100,32]{1,2,0:T(8,128)(2,1)S(1)} %convert_element_type.78), channel_id=1, replica_groups=mesh['dp'=16,'rep'=2] {'dp'}, dimensions={2}, use_global_device_ids=true | all-gather | bytes 435200 | tf_op jit(solution)/shard_map/all_gather | solution.py:71
  96.2 6.9 copy.50
  103.1 6.7 gather_fusion
  109.8 0.5 copy.51
  110.3 0.2 gather.7
  110.5 4.5 fusion
  115.0 9.2 %copy.53 = f32[1024,2048]{1,0:T(8,128)} copy(f32[1024,2048]{0,1:T(8,128)} %bitcast.71) | data formatting | bytes 16777216 | tf_op jit(solution)/shard_map/reshape | solution.py:87
  124.2 37.0 %all-reduce.4 = (f32[2048]{0:T(1024)S(1)}, f32[2048]{0:T(1024)S(1)}) all-reduce(f32[2048]{0:T(1024)S(1)} %bitcast.97, f32[2048]{0:T(1024)S(1)} %bitcast.96), channel_id=1, replica_groups=mesh['dp'=16,'rep'=2] {'dp','rep'}, use_global_device_ids=true, to_apply=%region_3.4 | all-reduce | flops 4096 | bytes 32768 | tf_op jit(solution)/shard_map/psum | solution.py:88
  161.1 43.3 %all_gather.18 = bf16[512,47]{1,0:T(8,128)(2,1)} all-gather(bf16[32,47]{1,0:T(8,128)(2,1)S(1)} %convert_element_type.84), channel_id=1, replica_groups=mesh['dp'=16,'rep'=2] {'dp'}, dimensions={0}, use_global_device_ids=true | all-gather | bytes 51136 | tf_op jit(solution)/shard_map/all_gather | solution.py:73
  204.4 0.5 slice_bitcast_fusion.4
  204.9 0.6 fusion.31
  205.5 9.1 %add_convert_fusion = bf16[1024,2048]{1,0:T(8,128)(2,1)} fusion(f32[2048]{0:T(1024)S(1)} %get-tuple-element.89, f32[2048]{0:T(1024)S(1)} %bitcast.86, f32[2048]{0:T(1024)S(1)} %broadcast_subtract_fusion.1, f32[2048]{0:T(1024)S(1)} %bitcast.92, f32[2048]{0:T(1024)S(1)} %get-tuple-element.82, f32[1024,2048]{1,0:T(8,128)} %copy.53, ...), kind=kLoop, calls=%fused_computation.10 | loop fusion | flops 39845888 | bytes 12648448 | tf_op jit(solution)/shard_map/convert_element_type | solution.py:96
  214.7 5.2 multiply_reduce_fusion.5
  219.9 37.1 %all-reduce.3 = (f32[512]{0:T(512)}, f32[512]{0:T(512)}) all-reduce(f32[512]{0:T(512)S(1)} %get-tuple-element.40, f32[512]{0:T(512)S(1)} %get-tuple-element.39), channel_id=1, replica_groups=mesh['dp'=16,'rep'=2] {'dp','rep'}, use_global_device_ids=true, to_apply=%region_7.8 | all-reduce | flops 1024 | bytes 8192 | tf_op jit(solution)/shard_map/psum | solution.py:98
  256.9 0.7 add_rsqrt_fusion.1
  257.7 1.6 add_convert_fusion.1
  259.2 1.3 fusion.32
  260.7 1.4 fusion.30
  262.0 1.1 convolution_convert_fusion.1
  263.2 4.2 multiply_reduce_fusion.3
  267.4 0.6 copy-done.14
  268.0 0.6 convert.38
  268.6 41.4 %all-reduce.2 = (f32[512]{0:T(512)}, f32[512]{0:T(512)}) all-reduce(f32[512]{0:T(512)} %copy-done.14, f32[512]{0:T(512)} %copy-done.15), channel_id=1, replica_groups=mesh['dp'=16,'rep'=2] {'dp','rep'}, use_global_device_ids=true, to_apply=%region_13.14 | all-reduce | flops 1024 | bytes 8192 | tf_op jit(solution)/shard_map/psum | solution.py:119
  310.0 0.8 multiply_multiply_fusion.5
  310.9 2.7 multiply_convert_fusion.1
  313.6 3.8 convolution_convert_fusion
  317.4 13.9 %multiply_reduce_fusion = (bf16[2048]{0:T(1024)(128)(2,1)S(1)}, bf16[2048]{0:T(1024)(128)(2,1)S(1)}, f32[2048]{0:T(1024)S(1)}, f32[2048]{0:T(1024)S(1)}, f32[1024,2048]{1,0:T(8,128)}) fusion(f32[2048]{0:T(1024)S(1)} %broadcast_subtract_fusion.1, f32[2048]{0:T(1024)S(1)} %bitcast.93, f32[2048]{0:T(1024)S(1)} %get-tuple-element.82, ...), kind=kOutput, calls=%fused_computation.4 | convolution fusion | flops 2225070080 | bytes 20013056 | tf_op jit(solution)/shard_map/dot_general | solution.py:29
  331.3 40.2 %all-reduce.1 = (f32[2048]{0:T(1024)S(1)}, f32[2048]{0:T(1024)S(1)}) all-reduce(f32[2048]{0:T(1024)S(1)} %get-tuple-element.32, f32[2048]{0:T(1024)S(1)} %get-tuple-element.33), channel_id=1, replica_groups=mesh['dp'=16,'rep'=2] {'dp','rep'}, use_global_device_ids=true, to_apply=%region_17.18 | all-reduce | flops 4096 | bytes 32768 | tf_op jit(solution)/shard_map/psum | solution.py:134
  371.7 1.9 concatenate.6
  373.5 0.3 all-reduce.12.cloned.1.call-start
  373.8 7.3 multiply_convert_fusion
  381.1 1.9 copy-done
  383.0 2.5 fusion.10
  385.6 5.8 all-reduce.10.cloned.1.call-done
  391.4 1.6 copy.56
  393.1 1.6 convert_element_type.94
  394.8 23.1 %all-reduce.12.cloned.1.call-done = (bf16[4,100,512]{1,2,0:T(8,128)(2,1)}, bf16[2048,512]{1,0:T(8,128)(2,1)}) async-done(((bf16[4,100,512]{1,2,0:T(8,128)(2,1)}, bf16[2048,512]{1,0:T(8,128)(2,1)}), (bf16[4,100,512]{1,2,0:T(8,128)(2,1)}, bf16[2048,512]{1,0:T(8,128)(2,1)})) %all-reduce.12.cloned.1.call-update) | async-done | bytes 2506768 | tf_op jit(solution)/shard_map/psum | solution.py:165
  417.9 2.1 convert_element_type.90
  420.1 4.2 convert_element_type.92
  424.4 3.7 fusion.7
  428.1 69.9 %reduce-scatter.13.cloned.1.call-done = f32[32,20]{1,0:T(8,128)} async-done(((f32[512,20]{1,0:T(8,128)}), f32[32,20]{1,0:T(8,128)}) %reduce-scatter.13.cloned.1.call-update) | async-done | bytes 2576
  498.0 0.8 copy.57
  498.8 0.6 multiply_reduce_fusion.9
  499.4 73.8 %reduce-scatter.11.cloned.1.call-done = f32[32,47]{1,0:T(8,128)} async-done(((f32[512,47]{1,0:T(8,128)}), f32[32,47]{1,0:T(8,128)}) %reduce-scatter.11.cloned.1.call-update) | async-done | bytes 6032 | tf_op jit(solution)/shard_map/reduce_scatter | solution.py:173
  573.1 1.3 multiply_reduce_fusion.8
  574.5 75.5 %reduce-scatter.7.cloned.1.call-done = f32[4,100,32]{1,2,0:T(8,128)} async-done(((f32[4,100,512]{1,2,0:T(8,128)}), f32[4,100,32]{1,2,0:T(8,128)}) %reduce-scatter.7.cloned.1.call-update) | async-done | bytes 51216 | tf_op jit(solution)/shard_map/reduce_scatter | solution.py:171
  650.0 1.5 multiply_reduce_fusion.7
  651.5 92.4 %reduce-scatter.9.cloned.1.call-done = f32[128,512]{1,0:T(8,128)} async-done(((f32[2048,512]{1,0:T(8,128)}), f32[128,512]{1,0:T(8,128)}) %reduce-scatter.9.cloned.1.call-update) | async-done | bytes 262160 | tf_op jit(solution)/shard_map/reduce_scatter | solution.py:172
  743.9 1.7 multiply_reduce_fusion.6
  748.2 1.3 reshape.135
  749.5 40.5 %psum.103 = f32[]{:T(128)} all-reduce(f32[]{:T(128)S(6)} %add.234), channel_id=1, replica_groups=mesh['dp'=16,'rep'=2] {'dp'}, use_global_device_ids=true, to_apply=%region_34.35 | all-reduce | flops 1 | bytes 8 | tf_op jit(solution)/shard_map/psum | solution.py:179
  790.8 1.4 fusion.22
  792.2 1.4 fusion.24
  793.5 1.6 fusion.28
  795.1 1.1 fusion.26
  (83 shorter events, 0.6 us)
Async XLA Ops:
  7.2 207.5 %all-gather.3.cloned.1.call-start = ((), (), s32[]{:S(2)}) async-start(), calls=%async_computation.4 | async-start | bytes 2228224 | tf_op jit(solution)/shard_map/all_gather | solution.py:72
  8.9 382.5 %all-reduce.10.cloned.1.call-start = ((), (), s32[]{:S(2)}) async-start(), calls=%async_computation.9 | async-start | bytes 311296 | tf_op jit(solution)/shard_map/psum | solution.py:167
  9.6 100.9 %copy-start.16 = (pred[1024]{0:T(1024)(128)(4,1)}, pred[1024]{0:T(1024)(128)(4,1)S(1)}, u32[]{:S(2)}) copy-start(pred[1024]{0:T(1024)(128)(4,1)S(1)} %compare_and_fusion) | copy-start | bytes 3076
  256.9 6.2 copy-start.4
  267.4 0.6 copy-start.14
  267.4 1.1 copy-start.15
  310.0 3.5 copy-start.1
  310.8 6.5 slice-start
  313.5 3.8 slice-start.1
  313.6 3.8 copy-start.21
  317.4 54.2 %copy-start.20 = (bf16[512]{0:T(512)(128)(2,1)S(1)}, bf16[512]{0:T(512)(128)(2,1)}, u32[]{:S(2)}) copy-start(bf16[512]{0:T(512)(128)(2,1)} %get-tuple-element.36) | copy-start | bytes 3076
  317.4 54.2 %copy-start.18 = (bf16[512]{0:T(512)(128)(2,1)S(1)}, bf16[512]{0:T(512)(128)(2,1)}, u32[]{:S(2)}) copy-start(bf16[512]{0:T(512)(128)(2,1)} %convert.38) | copy-start | bytes 3076
  317.4 54.2 %copy-start.19 = (bf16[47]{0:T(256)(128)(2,1)S(1)}, bf16[47]{0:T(256)(128)(2,1)}, u32[]{:S(2)}) copy-start(bf16[47]{0:T(256)(128)(2,1)} %get-tuple-element.69) | copy-start | bytes 286
  373.5 44.4 %all-reduce.12.cloned.1.call-start = ((), (), s32[]{:S(2)}) async-start(), calls=%async_computation.10 | async-start | bytes 5242880 | tf_op jit(solution)/shard_map/psum | solution.py:165
  373.8 9.2 %copy-start.17 = (pred[1024]{0:T(1024)(128)(4,1)S(1)}, pred[1024]{0:T(1024)(128)(4,1)}, u32[]{:S(2)}) copy-start(pred[1024]{0:T(1024)(128)(4,1)} %copy-done.16) | copy-start | bytes 3076
  381.1 1.9 copy-start
  385.5 112.5 %reduce-scatter.13.cloned.1.call-start = ((), (), s32[]{:S(2)}) async-start(), calls=%async_computation.8 | async-start | bytes 278528
  393.0 180.1 %reduce-scatter.11.cloned.1.call-start = ((), (), s32[]{:S(2)}) async-start(), calls=%async_computation.7 | async-start | bytes 278528 | tf_op jit(solution)/shard_map/reduce_scatter | solution.py:173
  394.7 255.3 %reduce-scatter.7.cloned.1.call-start = ((), (), s32[]{:S(2)}) async-start(), calls=%async_computation.5 | async-start | bytes 1114112 | tf_op jit(solution)/shard_map/reduce_scatter | solution.py:171
  420.0 323.9 %reduce-scatter.9.cloned.1.call-start = ((), (), s32[]{:S(2)}) async-start(), calls=%async_computation.6 | async-start | bytes 4456448 | tf_op jit(solution)/shard_map/reduce_scatter | solution.py:172
  424.2 366.6 %copy-start.11 = (f32[20,32]{1,0:T(8,128)S(1)}, f32[20,32]{1,0:T(8,128)}, u32[]{:S(2)}) copy-start(f32[20,32]{1,0:T(8,128)} %param.23) | copy-start | bytes 7684
  424.2 367.9 %copy-start.10 = (f32[32,47]{1,0:T(8,128)S(1)}, f32[32,47]{1,0:T(8,128)}, u32[]{:S(2)}) copy-start(f32[32,47]{1,0:T(8,128)} %param.22) | copy-start | bytes 18052
  424.3 367.9 %copy-start.12 = (f32[32,47]{1,0:T(8,128)S(1)}, f32[32,47]{1,0:T(8,128)}, u32[]{:S(2)}) copy-start(f32[32,47]{1,0:T(8,128)} %param.26) | copy-start | bytes 18052
  424.3 367.9 %copy-start.13 = (f32[32,47]{1,0:T(8,128)S(1)}, f32[32,47]{1,0:T(8,128)}, u32[]{:S(2)}) copy-start(f32[32,47]{1,0:T(8,128)} %param.30) | copy-start | bytes 18052
  424.3 369.3 %copy-start.7 = (f32[4,100,32]{1,2,0:T(8,128)S(1)}, f32[4,100,32]{1,2,0:T(8,128)}, u32[]{:S(2)}) copy-start(f32[4,100,32]{1,2,0:T(8,128)} %param.20) | copy-start | bytes 153604
  424.3 369.2 %copy-start.8 = (f32[4,100,32]{1,2,0:T(8,128)S(1)}, f32[4,100,32]{1,2,0:T(8,128)}, u32[]{:S(2)}) copy-start(f32[4,100,32]{1,2,0:T(8,128)} %param.24) | copy-start | bytes 153604
  424.3 369.2 %copy-start.9 = (f32[4,100,32]{1,2,0:T(8,128)S(1)}, f32[4,100,32]{1,2,0:T(8,128)}, u32[]{:S(2)}) copy-start(f32[4,100,32]{1,2,0:T(8,128)} %param.28) | copy-start | bytes 153604
  424.3 370.8 %copy-start.2 = (f32[128,512]{1,0:T(8,128)S(1)}, f32[128,512]{1,0:T(8,128)}, u32[]{:S(2)}) copy-start(f32[128,512]{1,0:T(8,128)} %param.21) | copy-start | bytes 786436
  424.3 370.8 %copy-start.5 = (f32[128,512]{1,0:T(8,128)S(1)}, f32[128,512]{1,0:T(8,128)}, u32[]{:S(2)}) copy-start(f32[128,512]{1,0:T(8,128)} %param.25) | copy-start | bytes 786436
  424.3 370.8 %copy-start.6 = (f32[128,512]{1,0:T(8,128)S(1)}, f32[128,512]{1,0:T(8,128)}, u32[]{:S(2)}) copy-start(f32[128,512]{1,0:T(8,128)} %param.29) | copy-start | bytes 786436
  743.9 51.2 %copy-start.3 = (f32[128,512]{1,0:T(8,128)S(1)}, f32[128,512]{1,0:T(8,128)}, u32[]{:S(2)}) copy-start(f32[128,512]{1,0:T(8,128)} %reduce-scatter.9.cloned.1.call-done) | copy-start | bytes 786436
Sparse Core Ops, SparseCore 0:
  11.4 66.4 all-gather.2
  373.7 17.7 all-reduce.9
  394.4 23.4 all-reduce.11
  420.7 77.2 reduce-scatter.12
  500.6 72.4 reduce-scatter.10
  575.9 74.0 reduce-scatter.6
  652.3 91.5 reduce-scatter.8
where the time goes:
time: 806 us; the launch traced here: 804 us
  waiting for transfers between devices  341 us (42%)
  blocking collectives  323 us (40%)
  other arithmetic  48.4 us (6%)
  matrix products  40.3 us (5%)
  local copies, waits for them, and re-layouts  32.3 us (4%)
  between operations  19 us (2%)
    reduce_scatter x1, waiting for transfers between devices, on_device(): lax.psum_scatter(paired[1], 'dp', scatter_dimension=0, tiled=True)  92.4 us
    reduce_scatter x1, waiting for transfers between devices, on_device(): lax.psum_scatter(paired[0], 'dp', scatter_dimension=2, tiled=True)  75.5 us
    reduce_scatter x1, waiting for transfers between devices, on_device(): lax.psum_scatter(paired[2], 'dp', scatter_dimension=0, tiled=True)  73.8 us
    unnamed x8, waiting for transfers between devices  70 us
    all_gather x1, blocking collectives, on_device(): lax.all_gather(w_class.astype(jnp.bfloat16), 'dp', axis=0, tiled=True)  43.3 us
    all_gather x1, blocking collectives, on_device(): lax.all_gather(small_params.astype(jnp.bfloat16), 'dp', axis=1, tiled=True)  43 us
    psum x1, blocking collectives, on_device(): totals_two = lax.psum((shift2_part, gain2_part), ('dp', 'rep'))  41.4 us
    psum x1, blocking collectives, on_device(): grad_norm = jnp.sqrt(lax.psum(local_squares, 'dp'))  40.5 us
  transfers between devices with their start and end apart: 7, of which 6 were waited for; matrix products, arithmetic and copies ran while one was open for 9% of the time, Pallas kernels for 0%

commit v1 on v0

--- a/solution.py
+++ b/solution.py
@@ -1,3 +1,4 @@
+import functools
 import jax
 import jax.numpy as jnp
 from jax import lax
@@ -6,6 +7,13 @@
 HOPS = 4
 STEP = 7
 EPS_NORM = 1e-05
+
+
+def show_signs(load, along_axis, axis_name):
+    return lax.psum(lax.psum(load, along_axis), axis_name)
+
+
+direct_teams_here = functools.partial(show_signs, along_axis="rep", axis_name="dp")
 
 
 def leaky(value, slope):
@@ -85,8 +93,8 @@
     first_pre = jnp.einsum(
         "fsq,sqv->fsv", input_features, branch_full, preferred_element_type=jnp.float32
     ).reshape(batch, hidden_width)
-    sums_one = lax.psum(
-        (jnp.sum(first_pre, axis=0), jnp.sum(first_pre * first_pre, axis=0)), ("dp", "rep")
+    sums_one = direct_teams_here(
+        (jnp.sum(first_pre, axis=0), jnp.sum(first_pre * first_pre, axis=0))
     )
     mean1 = sums_one[0] / row_count
     inv1 = lax.rsqrt(sums_one[1] / row_count - mean1 * mean1 + EPS_NORM)

time: 806 us -> 842 us (1.045)
  blocking collectives: 323 us -> 358 us
    psum x1 -> x2, blocking collectives: 37 us -> 76.2 us  [show_signs(): return lax.psum(lax.psum(load, along_axis), axis_name)]
  transfers between devices with their start and end apart: 7 -> 7, of which waited for: 6 -> 6; matrix products, arithmetic and copies ran while one was open for 9% -> 8% of each run, Pallas kernels for 0% -> 0%
where the time goes in v1:
time: 842 us; the launch traced here: 840 us
  blocking collectives  358 us (43%)
  waiting for transfers between devices  342 us (41%)
  other arithmetic  48.3 us (6%)
  matrix products  40.3 us (5%)
  local copies, waits for them, and re-layouts  32.3 us (4%)
  between operations  19 us (2%)
    reduce_scatter x1, waiting for transfers between devices, on_device(): lax.psum_scatter(paired[1], 'dp', scatter_dimension=0, tiled=True)  92.4 us
    psum x2, blocking collectives, show_signs(): return lax.psum(lax.psum(load, along_axis), axis_name)  76.2 us
    reduce_scatter x1, waiting for transfers between devices, on_device(): lax.psum_scatter(paired[0], 'dp', scatter_dimension=2, tiled=True)  75.5 us
    reduce_scatter x1, waiting for transfers between devices, on_device(): lax.psum_scatter(paired[2], 'dp', scatter_dimension=0, tiled=True)  73.8 us
    unnamed x8, waiting for transfers between devices  70 us
    psum x1, blocking collectives, on_device(): totals_two = lax.psum((shift2_part, gain2_part), ('dp', 'rep'))  43.3 us
    all_gather x1, blocking collectives, on_device(): lax.all_gather(small_params.astype(jnp.bfloat16), 'dp', axis=1, tiled=True)  43 us
    psum x1, blocking collectives, on_device(): grad_norm = jnp.sqrt(lax.psum(local_squares, 'dp'))  40.5 us
  transfers between devices with their start and end apart: 7, of which 6 were waited for; matrix products, arithmetic and copies ran while one was open for 8% of the time, Pallas kernels for 0%

profile of v1, /device:TPU:0, one launch (start us, length us, event | category | flops | bytes accessed | tf_op | source)
XLA Modules:
  0.0 840.0 jit_solution(15525753565361994493)
XLA Ops:
  7.2 1.6 convert_element_type.82
  8.9 0.7 compare_and_fusion
  9.6 0.7 fusion.19
  10.3 0.7 convert_bitcast_fusion
  11.0 0.7 convert_element_type.84
  11.8 0.8 convert_element_type.78
  12.6 43.0 %all-gather = bf16[16,32,20]{1,2,0:T(8,128)(2,1)S(1)} all-gather(bf16[1,32,20]{1,2,0:T(8,128)(2,1)S(1)} %convert_bitcast_fusion), channel_id=1, replica_groups=mesh['dp'=16,'rep'=2] {'dp'}, dimensions={0}, use_global_device_ids=true | all-gather | bytes 21760 | tf_op jit(solution)/shard_map/all_gather | solution.py:82
  55.6 0.1 reshape.147
  55.8 40.4 %all_gather.15 = bf16[4,100,512]{1,2,0:T(8,128)(2,1)S(1)} all-gather(bf16[4,100,32]{1,2,0:T(8,128)(2,1)S(1)} %convert_element_type.78), channel_id=1, replica_groups=mesh['dp'=16,'rep'=2] {'dp'}, dimensions={2}, use_global_device_ids=true | all-gather | bytes 435200 | tf_op jit(solution)/shard_map/all_gather | solution.py:79
  96.2 6.9 copy.50
  103.1 6.7 gather_fusion
  109.8 0.5 copy.51
  110.3 0.2 gather.7
  110.5 4.5 fusion
  115.0 9.2 %copy.53 = f32[1024,2048]{1,0:T(8,128)} copy(f32[1024,2048]{0,1:T(8,128)} %bitcast.71) | data formatting | bytes 16777216 | tf_op jit(solution)/shard_map/reshape | solution.py:95
  124.2 3.3 all-reduce.5
  127.4 72.9 %all-reduce.4 = (f32[2048]{0:T(1024)S(1)}, f32[2048]{0:T(1024)S(1)}) all-reduce(f32[2048]{0:T(1024)S(1)} %get-tuple-element.49, f32[2048]{0:T(1024)S(1)} %get-tuple-element.50), channel_id=1, replica_groups=mesh['dp'=16,'rep'=2] {'dp'}, use_global_device_ids=true, to_apply=%region_5.6 | all-reduce | flops 4096 | bytes 32768 | tf_op jit(solution)/shard_map/psum | solution.py:13
  200.4 38.5 %all_gather.18 = bf16[512,47]{1,0:T(8,128)(2,1)} all-gather(bf16[32,47]{1,0:T(8,128)(2,1)S(1)} %convert_element_type.84), channel_id=1, replica_groups=mesh['dp'=16,'rep'=2] {'dp'}, dimensions={0}, use_global_device_ids=true | all-gather | bytes 51136 | tf_op jit(solution)/shard_map/all_gather | solution.py:81
  238.8 0.5 slice_bitcast_fusion.4
  239.3 0.6 fusion.31
  239.9 9.1 %add_convert_fusion = bf16[1024,2048]{1,0:T(8,128)(2,1)} fusion(f32[2048]{0:T(1024)S(1)} %get-tuple-element.91, f32[2048]{0:T(1024)S(1)} %bitcast.86, f32[2048]{0:T(1024)S(1)} %broadcast_subtract_fusion.1, f32[2048]{0:T(1024)S(1)} %bitcast.92, f32[2048]{0:T(1024)S(1)} %get-tuple-element.84, f32[1024,2048]{1,0:T(8,128)} %copy.53, ...), kind=kLoop, calls=%fused_computation.10 | loop fusion | flops 39845888 | bytes 12648448 | tf_op jit(solution)/shard_map/convert_element_type | solution.py:104
  249.1 5.2 multiply_reduce_fusion.5
  254.3 37.1 %all-reduce.3 = (f32[512]{0:T(512)}, f32[512]{0:T(512)}) all-reduce(f32[512]{0:T(512)S(1)} %get-tuple-element.40, f32[512]{0:T(512)S(1)} %get-tuple-element.39), channel_id=1, replica_groups=mesh['dp'=16,'rep'=2] {'dp','rep'}, use_global_device_ids=true, to_apply=%region_9.10 | all-reduce | flops 1024 | bytes 8192 | tf_op jit(solution)/shard_map/psum | solution.py:106
  291.4 0.7 add_rsqrt_fusion.1
  292.1 1.6 add_convert_fusion.1
  293.7 1.3 fusion.32
  295.1 1.4 fusion.30
  296.4 1.1 convolution_convert_fusion.1
  297.6 4.2 multiply_reduce_fusion.3
  301.8 0.6 copy-done.14
  302.4 0.6 convert.38
  303.0 43.3 %all-reduce.2 = (f32[512]{0:T(512)}, f32[512]{0:T(512)}) all-reduce(f32[512]{0:T(512)} %copy-done.14, f32[512]{0:T(512)} %copy-done.15), channel_id=1, replica_groups=mesh['dp'=16,'rep'=2] {'dp','rep'}, use_global_device_ids=true, to_apply=%region_15.16 | all-reduce | flops 1024 | bytes 8192 | tf_op jit(solution)/shard_map/psum | solution.py:127
  346.3 0.8 multiply_multiply_fusion.5
  347.2 2.7 multiply_convert_fusion.1
  349.9 3.8 convolution_convert_fusion
  353.7 13.9 %multiply_reduce_fusion = (bf16[2048]{0:T(1024)(128)(2,1)S(1)}, bf16[2048]{0:T(1024)(128)(2,1)S(1)}, f32[2048]{0:T(1024)S(1)}, f32[2048]{0:T(1024)S(1)}, f32[1024,2048]{1,0:T(8,128)}) fusion(f32[2048]{0:T(1024)S(1)} %broadcast_subtract_fusion.1, f32[2048]{0:T(1024)S(1)} %bitcast.93, f32[2048]{0:T(1024)S(1)} %get-tuple-element.84, ...), kind=kOutput, calls=%fused_computation.4 | convolution fusion | flops 2225070080 | bytes 20013056 | tf_op jit(solution)/shard_map/dot_general | solution.py:37
  367.6 38.5 %all-reduce.1 = (f32[2048]{0:T(1024)S(1)}, f32[2048]{0:T(1024)S(1)}) all-reduce(f32[2048]{0:T(1024)S(1)} %get-tuple-element.32, f32[2048]{0:T(1024)S(1)} %get-tuple-element.33), channel_id=1, replica_groups=mesh['dp'=16,'rep'=2] {'dp','rep'}, use_global_device_ids=true, to_apply=%region_19.20 | all-reduce | flops 4096 | bytes 32768 | tf_op jit(solution)/shard_map/psum | solution.py:142
  406.2 1.9 concatenate.6
  408.1 0.3 all-reduce.13.cloned.1.call-start
  408.4 7.2 multiply_convert_fusion
  415.6 1.9 copy-done
  417.6 2.5 fusion.10
  420.1 7.2 all-reduce.11.cloned.1.call-done
  427.3 1.6 copy.56
  428.9 1.6 convert_element_type.94
  430.6 23.1 %all-reduce.13.cloned.1.call-done = (bf16[4,100,512]{1,2,0:T(8,128)(2,1)}, bf16[2048,512]{1,0:T(8,128)(2,1)}) async-done(((bf16[4,100,512]{1,2,0:T(8,128)(2,1)}, bf16[2048,512]{1,0:T(8,128)(2,1)}), (bf16[4,100,512]{1,2,0:T(8,128)(2,1)}, bf16[2048,512]{1,0:T(8,128)(2,1)})) %all-reduce.13.cloned.1.call-update) | async-done | bytes 2506768 | tf_op jit(solution)/shard_map/psum | solution.py:173
  453.7 2.1 convert_element_type.90
  455.9 4.2 convert_element_type.92
  460.2 3.7 fusion.7
  463.9 69.9 %reduce-scatter.13.cloned.1.call-done = f32[32,20]{1,0:T(8,128)} async-done(((f32[512,20]{1,0:T(8,128)}), f32[32,20]{1,0:T(8,128)}) %reduce-scatter.13.cloned.1.call-update) | async-done | bytes 2576
  533.8 0.8 copy.57
  534.6 0.6 multiply_reduce_fusion.9
  535.2 73.8 %reduce-scatter.11.cloned.1.call-done = f32[32,47]{1,0:T(8,128)} async-done(((f32[512,47]{1,0:T(8,128)}), f32[32,47]{1,0:T(8,128)}) %reduce-scatter.11.cloned.1.call-update) | async-done | bytes 6032 | tf_op jit(solution)/shard_map/reduce_scatter | solution.py:181
  609.0 1.3 multiply_reduce_fusion.8
  610.3 75.5 %reduce-scatter.7.cloned.1.call-done = f32[4,100,32]{1,2,0:T(8,128)} async-done(((f32[4,100,512]{1,2,0:T(8,128)}), f32[4,100,32]{1,2,0:T(8,128)}) %reduce-scatter.7.cloned.1.call-update) | async-done | bytes 51216 | tf_op jit(solution)/shard_map/reduce_scatter | solution.py:179
  685.8 1.5 multiply_reduce_fusion.7
  687.3 92.4 %reduce-scatter.9.cloned.1.call-done = f32[128,512]{1,0:T(8,128)} async-done(((f32[2048,512]{1,0:T(8,128)}), f32[128,512]{1,0:T(8,128)}) %reduce-scatter.9.cloned.1.call-update) | async-done | bytes 262160 | tf_op jit(solution)/shard_map/reduce_scatter | solution.py:180
  779.7 1.7 multiply_reduce_fusion.6
  784.0 1.3 reshape.135
  785.4 40.5 %psum.119 = f32[]{:T(128)} all-reduce(f32[]{:T(128)S(6)} %add.238), channel_id=1, replica_groups=mesh['dp'=16,'rep'=2] {'dp'}, use_global_device_ids=true, to_apply=%region_36.37 | all-reduce | flops 1 | bytes 8 | tf_op jit(solution)/shard_map/psum | solution.py:187
  826.6 1.4 fusion.22
  828.0 1.4 fusion.24
  829.4 1.6 fusion.28
  831.0 1.1 fusion.26
  (84 shorter events, 0.7 us)
Async XLA Ops:
  7.2 241.9 %all-gather.3.cloned.1.call-start = ((), (), s32[]{:S(2)}) async-start(), calls=%async_computation.4 | async-start | bytes 2228224 | tf_op jit(solution)/shard_map/all_gather | solution.py:80
  8.9 418.4 %all-reduce.11.cloned.1.call-start = ((), (), s32[]{:S(2)}) async-start(), calls=%async_computation.9 | async-start | bytes 311296 | tf_op jit(solution)/shard_map/psum | solution.py:175
  9.6 100.9 %copy-start.16 = (pred[1024]{0:T(1024)(128)(4,1)}, pred[1024]{0:T(1024)(128)(4,1)S(1)}, u32[]{:S(2)}) copy-start(pred[1024]{0:T(1024)(128)(4,1)S(1)} %compare_and_fusion) | copy-start | bytes 3076
  291.3 6.2 copy-start.4
  301.8 0.6 copy-start.14
  301.8 1.1 copy-start.15
  346.3 3.5 copy-start.1
  347.2 6.5 slice-start
  349.8 3.8 slice-start.1
  349.9 3.8 copy-start.21
  353.7 52.4 %copy-start.20 = (bf16[512]{0:T(512)(128)(2,1)S(1)}, bf16[512]{0:T(512)(128)(2,1)}, u32[]{:S(2)}) copy-start(bf16[512]{0:T(512)(128)(2,1)} %get-tuple-element.36) | copy-start | bytes 3076
  353.7 52.4 %copy-start.18 = (bf16[512]{0:T(512)(128)(2,1)S(1)}, bf16[512]{0:T(512)(128)(2,1)}, u32[]{:S(2)}) copy-start(bf16[512]{0:T(512)(128)(2,1)} %convert.38) | copy-start | bytes 3076
  353.7 52.5 %copy-start.19 = (bf16[47]{0:T(256)(128)(2,1)S(1)}, bf16[47]{0:T(256)(128)(2,1)}, u32[]{:S(2)}) copy-start(bf16[47]{0:T(256)(128)(2,1)} %get-tuple-element.71) | copy-start | bytes 286
  408.1 45.6 %all-reduce.13.cloned.1.call-start = ((), (), s32[]{:S(2)}) async-start(), calls=%async_computation.10 | async-start | bytes 5242880 | tf_op jit(solution)/shard_map/psum | solution.py:173
  408.4 9.2 %copy-start.17 = (pred[1024]{0:T(1024)(128)(4,1)S(1)}, pred[1024]{0:T(1024)(128)(4,1)}, u32[]{:S(2)}) copy-start(pred[1024]{0:T(1024)(128)(4,1)} %copy-done.16) | copy-start | bytes 3076
  415.6 1.9 copy-start
  420.0 113.8 %reduce-scatter.13.cloned.1.call-start = ((), (), s32[]{:S(2)}) async-start(), calls=%async_computation.8 | async-start | bytes 278528
  428.8 180.1 %reduce-scatter.11.cloned.1.call-start = ((), (), s32[]{:S(2)}) async-start(), calls=%async_computation.7 | async-start | bytes 278528 | tf_op jit(solution)/shard_map/reduce_scatter | solution.py:181
  430.5 255.3 %reduce-scatter.7.cloned.1.call-start = ((), (), s32[]{:S(2)}) async-start(), calls=%async_computation.5 | async-start | bytes 1114112 | tf_op jit(solution)/shard_map/reduce_scatter | solution.py:179
  455.8 323.9 %reduce-scatter.9.cloned.1.call-start = ((), (), s32[]{:S(2)}) async-start(), calls=%async_computation.6 | async-start | bytes 4456448 | tf_op jit(solution)/shard_map/reduce_scatter | solution.py:180
  460.1 366.6 %copy-start.11 = (f32[20,32]{1,0:T(8,128)S(1)}, f32[20,32]{1,0:T(8,128)}, u32[]{:S(2)}) copy-start(f32[20,32]{1,0:T(8,128)} %param.23) | copy-start | bytes 7684
  460.1 367.9 %copy-start.10 = (f32[32,47]{1,0:T(8,128)S(1)}, f32[32,47]{1,0:T(8,128)}, u32[]{:S(2)}) copy-start(f32[32,47]{1,0:T(8,128)} %param.22) | copy-start | bytes 18052
  460.1 367.9 %copy-start.12 = (f32[32,47]{1,0:T(8,128)S(1)}, f32[32,47]{1,0:T(8,128)}, u32[]{:S(2)}) copy-start(f32[32,47]{1,0:T(8,128)} %param.26) | copy-start | bytes 18052
  460.1 367.9 %copy-start.13 = (f32[32,47]{1,0:T(8,128)S(1)}, f32[32,47]{1,0:T(8,128)}, u32[]{:S(2)}) copy-start(f32[32,47]{1,0:T(8,128)} %param.30) | copy-start | bytes 18052
  460.1 369.3 %copy-start.7 = (f32[4,100,32]{1,2,0:T(8,128)S(1)}, f32[4,100,32]{1,2,0:T(8,128)}, u32[]{:S(2)}) copy-start(f32[4,100,32]{1,2,0:T(8,128)} %param.20) | copy-start | bytes 153604
  460.1 369.2 %copy-start.8 = (f32[4,100,32]{1,2,0:T(8,128)S(1)}, f32[4,100,32]{1,2,0:T(8,128)}, u32[]{:S(2)}) copy-start(f32[4,100,32]{1,2,0:T(8,128)} %param.24) | copy-start | bytes 153604
  460.1 369.2 %copy-start.9 = (f32[4,100,32]{1,2,0:T(8,128)S(1)}, f32[4,100,32]{1,2,0:T(8,128)}, u32[]{:S(2)}) copy-start(f32[4,100,32]{1,2,0:T(8,128)} %param.28) | copy-start | bytes 153604
  460.2 370.8 %copy-start.2 = (f32[128,512]{1,0:T(8,128)S(1)}, f32[128,512]{1,0:T(8,128)}, u32[]{:S(2)}) copy-start(f32[128,512]{1,0:T(8,128)} %param.21) | copy-start | bytes 786436
  460.2 370.8 %copy-start.5 = (f32[128,512]{1,0:T(8,128)S(1)}, f32[128,512]{1,0:T(8,128)}, u32[]{:S(2)}) copy-start(f32[128,512]{1,0:T(8,128)} %param.25) | copy-start | bytes 786436
  460.2 370.8 %copy-start.6 = (f32[128,512]{1,0:T(8,128)S(1)}, f32[128,512]{1,0:T(8,128)}, u32[]{:S(2)}) copy-start(f32[128,512]{1,0:T(8,128)} %param.29) | copy-start | bytes 786436
  779.7 51.2 %copy-start.3 = (f32[128,512]{1,0:T(8,128)S(1)}, f32[128,512]{1,0:T(8,128)}, u32[]{:S(2)}) copy-start(f32[128,512]{1,0:T(8,128)} %reduce-scatter.9.cloned.1.call-done) | copy-start | bytes 786436
Sparse Core Ops, SparseCore 0:
  11.4 66.4 all-gather.2
  408.2 18.9 all-reduce.10
  430.2 23.4 all-reduce.12
  456.5 77.2 reduce-scatter.12
  536.5 72.4 reduce-scatter.10
  611.8 74.0 reduce-scatter.6
  688.1 91.5 reduce-scatter.8
